TPU v7x, 512 devices: a whole 4x4x16 slice. The times are simulated.
512 devices in a mesh: dp: 16 (over z), retr: 8 (over x, core), fsdp: 4 (over y).
Axes of the slice: x: 4, y: 4, z: 16, core: 2. Of those that a mesh axis runs over, the one named last changes fastest.
Arguments:
- queries: bfloat16 [65536, 2048], P(('dp', 'retr', 'fsdp')), may hold values from -110 to 110, as said below
- encodings: bfloat16 [2048, 128, 896], P(('dp', 'retr', 'fsdp')), may hold values from -6 to 6
- owner_ids: int32 [1024, 2], P(('dp', 'retr', 'fsdp')), may hold values from 0 to 7, all different within a row; in each aligned block of 2 rows (0 to 1, 2 to 3, ...) at most 2 rows name the same one
- local_ids: int32 [1024, 2], P(('dp', 'retr', 'fsdp')), may hold values from 0 to 3
- key_weight: bfloat16 [896, 2048], P(('dp', 'fsdp')), may hold values from -0.1875 to 0.1875
- value_weight: bfloat16 [896, 2048], P(('dp', 'fsdp')), may hold values from -0.1875 to 0.1875
Outputs:
- attended: bfloat16 [65536, 2048], P(('dp', 'retr', 'fsdp'))
Inputs may be any that keep to these rules, and one draw needn't show every extreme that they name: `queries`: entries are bounded. `owner_ids`: the two neighbours of a stretch have different owners; among the stretches of one device no owner is named more than 2 times, and in every draw some device's stretches name some owner exactly 2 times.
All inputs are finite; a program needn't handle non-finite values.
Results may differ from a plain program's by a relative error of at most 0.011.
Values may be sent and summed in bfloat16 or wider, within the bound.
No kernel may reach another device: no remote copies, remote signals or barrier semaphores. Data moves between devices by JAX's collectives and lax.ppermute only.
A program may use at most 64 MiB of HBM per device.

v0:
```python
import math
import jax
import jax.numpy as jnp
from jax import lax
from jax.sharding import PartitionSpec as P

HEADS = 16
STRETCH = 64


def passed_along(block, axis, distance):
    devices = range(lax.axis_size(axis))
    route = [(i - distance, i) for i in devices if i - distance in devices]
    return lax.ppermute(block, axis, route)


def body(queries, encodings, owner_ids, local_ids, key_weight, value_weight):
    tokens = queries.shape[0]
    columns = queries.shape[1]
    head_size = columns // HEADS
    stretches = tokens // STRETCH
    neighbours = owner_ids.shape[1]
    slot_count = stretches * neighbours
    owners = owner_ids.reshape(slot_count)
    places = local_ids.reshape(slot_count)
    gathered = lax.all_gather(encodings, "retr", axis=0, tiled=True)
    fetched = jnp.take(gathered, owners * encodings.shape[0] + places, axis=0)
    span = neighbours * encodings.shape[1]
    panel_rows = fetched.reshape(stretches * span, encodings.shape[2])
    key_full, value_full = (
        lax.all_gather(key_weight, ("dp", "fsdp"), axis=0, tiled=True),
        lax.all_gather(value_weight, ("dp", "fsdp"), axis=0, tiled=True),
    )
    prior_rows = passed_along(panel_rows[(stretches - 1) * span :], "fsdp", 1)
    every_row = jnp.concatenate([prior_rows, panel_rows], 0)
    key_block = jnp.dot(every_row, key_full, preferred_element_type=jnp.float32).astype(
        jnp.bfloat16
    )
    value_block = jnp.dot(every_row, value_full, preferred_element_type=jnp.float32).astype(
        jnp.bfloat16
    )
    key_block = key_block.reshape(stretches + 1, span, columns)
    value_block = value_block.reshape(stretches + 1, span, columns)
    padded = jnp.concatenate(
        [
            jnp.zeros((1, columns), jnp.bfloat16),
            queries,
            jnp.zeros((STRETCH - 1, columns), jnp.bfloat16),
        ],
        0,
    )
    query_block = padded.reshape(stretches + 1, STRETCH, HEADS, head_size)
    key_heads = key_block.reshape(stretches + 1, span, HEADS, head_size)
    value_heads = value_block.reshape(stretches + 1, span, HEADS, head_size)
    scores = jnp.einsum(
        "cqhd,ckhd->chqk", query_block, key_heads, preferred_element_type=jnp.float32
    ) / math.sqrt(head_size)
    probs = jax.nn.softmax(scores, axis=-1).astype(jnp.bfloat16)
    result = jnp.einsum(
        "chqk,ckhd->cqhd", probs, value_heads, preferred_element_type=jnp.float32
    ).astype(jnp.bfloat16)
    result = result.reshape((stretches + 1) * STRETCH, columns)[1 : tokens + 1]
    follower = lax.axis_index("fsdp") > 0
    position = jnp.arange(tokens, dtype=jnp.int32)
    visible = follower | (position >= STRETCH - 1)
    return jnp.where(visible[:, None], result, jnp.zeros_like(result))


def solution(mesh):
    in_specs = (
        P(("dp", "retr", "fsdp"), None),
        P(("dp", "retr", "fsdp"), None, None),
        P(("dp", "retr", "fsdp"), None),
        P(("dp", "retr", "fsdp"), None),
        P(("dp", "fsdp"), None),
        P(("dp", "fsdp"), None),
    )
    out_specs = P(("dp", "retr", "fsdp"), None)
    return jax.shard_map(body, mesh=mesh, in_specs=in_specs, out_specs=out_specs, check_vma=False)
```

profile of v0, /device:TPU:2, one launch (start us, length us, event | category | flops | bytes accessed | tf_op | source)
XLA Modules:
  0.0 400.2 jit_solution(17860496296428153999)
XLA Ops:
  6.5 0.7 all-gather.6.cloned.1.call-update
  7.3 0.7 all-gather.8.cloned.1.call-update
  8.0 0.0 all-gather.10.cloned.1.call-start
  8.1 0.7 all-gather.10.cloned.1.call-update
  8.7 0.7 multiply_add_fusion
  9.4 0.1 add.36
  9.5 0.1 add.34
  9.6 0.1 slice.14
  9.7 0.1 pad.4.clone
  9.8 1.4 maximum_bitcast_fusion
  11.2 1.1 copy.17
  12.3 53.7 %all-gather.6.cloned.1.call-done = bf16[32,128,896]{2,1,0:T(8,128)(2,1)} async-done(((bf16[4,128,896]{2,1,0:T(8,128)(2,1)}), bf16[32,128,896]{2,1,0:T(8,128)(2,1)}) %all-gather.6.cloned.1.call-update) | async-done | bytes 7340048 | tf_op jit(solution)/shard_map/all_gather | solution.py:26
  66.0 3.8 gather_fusion
  69.8 0.1 slice_select_fusion.1
  69.9 3.4 collective-permute-start
  73.3 0.1 broadcast_bitcast_fusion
  73.4 142.8 %all-gather.8.cloned.1.call-done = bf16[64,14,2048]{2,1,0:T(8,128)(2,1)} async-done(((bf16[1,14,2048]{2,1,0:T(8,128)(2,1)}), bf16[64,14,2048]{2,1,0:T(8,128)(2,1)}) %all-gather.8.cloned.1.call-update) | async-done | bytes 3670032 | tf_op jit(solution)/shard_map/all_gather | solution.py:32
  216.3 6.0 %reshape.73 = bf16[896,2048]{1,0:T(8,128)(2,1)} reshape(bf16[64,14,2048]{2,1,0:T(8,128)(2,1)} %all-gather.8.cloned.1.call-done) | data formatting | bytes 7340032
  222.2 137.9 %all-gather.10.cloned.1.call-done = bf16[64,14,2048]{2,1,0:T(8,128)(2,1)} async-done(((bf16[1,14,2048]{2,1,0:T(8,128)(2,1)}), bf16[64,14,2048]{2,1,0:T(8,128)(2,1)}) %all-gather.10.cloned.1.call-update) | async-done | bytes 3670032 | tf_op jit(solution)/shard_map/all_gather | solution.py:31
  360.1 6.0 %reshape.75 = bf16[896,2048]{1,0:T(8,128)(2,1)} reshape(bf16[64,14,2048]{2,1,0:T(8,128)(2,1)} %all-gather.10.cloned.1.call-done) | data formatting | bytes 7340032
  366.2 0.2 bitcast_select_fusion
  366.4 6.0 %fusion.8 = bf16[96,8,16,128]{3,1,2,0:T(8,128)(2,1)S(1)} fusion(bf16[896,2048]{1,0:T(8,128)(2,1)} %reshape.73, bf16[512,896]{1,0:T(8,128)(2,1)S(1)} %bitcast_select_fusion, bf16[256,896]{1,0:T(8,128)(2,1)S(1)} %collective-permute-done), kind=kOutput, calls=%fused_computation.12 | convolution fusion | flops 2822897664 | bytes 8192000 | tf_op jit(solution)/shard_map/dot_general | solution.py:39
  372.5 2.7 copy.19
  375.2 4.0 fusion.9
  379.1 1.0 copy.18
  380.2 0.1 copy-done.1
  380.3 1.2 fusion.3
  381.5 1.1 fusion.30
  382.6 8.2 %fusion.15 = bf16[3,64,16,128]{3,1,2,0:T(8,128)(2,1)} fusion(bf16[3,256,16,128]{3,2,1,0:T(8,128)(2,1)} %bitcast.33, f32[3,16,64]{2,1,0:T(8,128)S(1)} %fusion.30, f32[3,16,64,256]{3,2,1,0:T(8,128)S(1)} %fusion.3), kind=kOutput, calls=%fused_computation.18 | convolution fusion | flops 205655296 | bytes 7090176 | tf_op jit(solution)/shard_map/chqk,ckhd->cqhd/dot_general | solution.py:59
  390.9 1.6 copy.16
  392.5 0.2 copy.32
  392.7 1.0 slice_select_fusion
  (12 shorter events, 0.1 us)
Async XLA Ops:
  6.5 59.5 %all-gather.6.cloned.1.call-start = ((), (), s32[]{:S(2)}) async-start(), calls=%async_computation | async-start | bytes 8257536 | tf_op jit(solution)/shard_map/all_gather | solution.py:26
  7.3 209.0 %all-gather.8.cloned.1.call-start = ((), (), s32[]{:S(2)}) async-start(), calls=%async_computation.1 | async-start | bytes 4259840 | tf_op jit(solution)/shard_map/all_gather | solution.py:32
  8.0 352.1 %all-gather.10.cloned.1.call-start = ((), (), s32[]{:S(2)}) async-start(), calls=%async_computation.2 | async-start | bytes 4259840 | tf_op jit(solution)/shard_map/all_gather | solution.py:31
  69.9 296.5 %collective-permute-start = (bf16[256,896]{1,0:T(8,128)(2,1)S(1)}, bf16[256,896]{1,0:T(8,128)(2,1)S(1)}, u32[]{:S(2)}, u32[]{:S(2)}) collective-permute-start(bf16[256,896]{1,0:T(8,128)(2,1)S(1)} %bitcast.36), channel_id=1, source_target_pairs={{0,1},{1,2},{2,3},{4,5},{5,6},{6,7},{8,9},{9,10},{10,11},{12,13},{... | collective-permute-start | bytes 1376264 | tf_op jit(solution)/shard_map/ppermute | solution.py:14
  372.5 2.7 copy-start
  379.1 1.1 copy-start.1
Sparse Core Ops, SparseCore 0:
  9.5 56.5 all-gather.5
  68.9 147.2 all-gather.7
  219.2 140.8 all-gather.9
where the time goes:
time: 401 us; the launch traced here: 400 us
  waiting for transfers between devices  337 us (84%)
  local copies, waits for them, and re-layouts  22.9 us (6%)
  matrix products  19.5 us (5%)
  between operations  13.2 us (3%)
  other arithmetic  4.63 us (1%)
    all_gather x1, waiting for transfers between devices, body(): lax.all_gather(value_weight, ('dp', 'fsdp'), axis=0, tiled=True)  143 us
    all_gather x1, waiting for transfers between devices, body(): lax.all_gather(key_weight, ('dp', 'fsdp'), axis=0, tiled=True)  138 us
    all_gather x1, waiting for transfers between devices, body(): gathered = lax.all_gather(encodings, 'retr', axis=0, tiled=True)  53.7 us
    unnamed x10, local copies, waits for them, and re-layouts  17.1 us
    dot_general x1, matrix products, body(): jnp.einsum('chqk,ckhd->cqhd', probs, value_heads, preferred_element_type=...  8.23 us
  transfers between devices with their start and end apart: 4, of which 3 were waited for; matrix products, arithmetic and copies ran while one was open for 5% of the time, Pallas kernels for 0%

commit v1 on v0

--- a/solution.py
+++ b/solution.py
@@ -6,6 +6,21 @@
 
 HEADS = 16
 STRETCH = 64
+
+
+def define_hubs(x_in):
+    n_axis = jax.lax.axis_size("retr")
+    samples = [(j, (j + 1) % n_axis) for j in range(n_axis)]
+    steps_seen = [(j, (j - 1) % n_axis) for j in range(n_axis)]
+    even, v_now = ([x_in], [x_in])
+    for _ in range(n_axis // 2):
+        even.append(jax.lax.ppermute(even[-1], axis_name="retr", perm=samples))
+    for _ in [*range((n_axis - 1) // 2)]:
+        v_now.append(jax.lax.ppermute(v_now[-1], perm=steps_seen, axis_name="retr"))
+    m_next = jnp.concatenate([*even[::-1], *v_now[1:]], axis=0)
+    return jnp.roll(
+        m_next, shift=(jax.lax.axis_index("retr") - n_axis // 2) * x_in.shape[0], axis=0
+    )
 
 
 def passed_along(block, axis, distance):
@@ -23,7 +38,7 @@
     slot_count = stretches * neighbours
     owners = owner_ids.reshape(slot_count)
     places = local_ids.reshape(slot_count)
-    gathered = lax.all_gather(encodings, "retr", axis=0, tiled=True)
+    gathered = define_hubs(encodings)
     fetched = jnp.take(gathered, owners * encodings.shape[0] + places, axis=0)
     span = neighbours * encodings.shape[1]
     panel_rows = fetched.reshape(stretches * span, encodings.shape[2])

time: 401 us -> 343 us (0.86)
  waiting for transfers between devices: 337 us -> 240 us
  local copies, waits for them, and re-layouts: 22.9 us -> 52.8 us
  starting transfers between devices: 3.5 us -> 9 us
    all_gather x1, waiting for transfers between devices: 138 us -> 62.9 us  [body(): lax.all_gather(key_weight, ('dp', 'fsdp'), axis=0, tiled=True)]
    all_gather x1 -> x0, waiting for transfers between devices: 53.7 us -> none  [body(): gathered = lax.all_gather(encodings, 'retr', axis=0, tiled=True)]
    ppermute x0 -> x7, waiting for transfers between devices: none -> 43.9 us  [the longest x4 43.9 us: define_hubs(): even.append(jax.lax.ppermute(even[-1], axis_name='retr', perm=samples))]
    unnamed x10 -> x25, local copies, waits for them, and re-layouts: 17.1 us -> 40.1 us
    all_gather x1, waiting for transfers between devices: 143 us -> 132 us  [body(): lax.all_gather(value_weight, ('dp', 'fsdp'), axis=0, tiled=True)]
    dynamic_slice x0 -> x1, local copies, waits for them, and re-layouts: none -> 6.97 us  [define_hubs(): jnp.roll(m_next, shift=(jax.lax.axis_index('retr') - n_axis // 2) * x_in....]
    ppermute x0 -> x7, starting transfers between devices: none -> 5.27 us  [the longest x3 5.25 us: define_hubs(): v_now.append(jax.lax.ppermute(v_now[-1], perm=steps_seen, axis_name='retr'))]
  transfers between devices with their start and end apart: 4 -> 10, of which waited for: 3 -> 6; matrix products, arithmetic and copies ran while one was open for 5% -> 15% of each run, Pallas kernels for 0% -> 0%
where the time goes in v1:
time: 343 us; the launch traced here: 342 us
  waiting for transfers between devices  240 us (70%)
  local copies, waits for them, and re-layouts  52.8 us (15%)
  matrix products  22.4 us (7%)
  between operations  13.6 us (4%)
  starting transfers between devices  9 us (3%)
  other arithmetic  4.68 us (1%)
    all_gather x1, waiting for transfers between devices, body(): lax.all_gather(value_weight, ('dp', 'fsdp'), axis=0, tiled=True)  132 us
    all_gather x1, waiting for transfers between devices, body(): lax.all_gather(key_weight, ('dp', 'fsdp'), axis=0, tiled=True)  62.9 us
    ppermute x4, waiting for transfers between devices, define_hubs(): even.append(jax.lax.ppermute(even[-1], axis_name='retr', perm=samples))  43.9 us
    unnamed x25, local copies, waits for them, and re-layouts  40.1 us
    dot_general x1, matrix products, body(): jnp.einsum('chqk,ckhd->cqhd', probs, value_heads, preferred_element_type=...  9.21 us
    dynamic_slice x1, local copies, waits for them, and re-layouts, define_hubs(): jnp.roll(m_next, shift=(jax.lax.axis_index('retr') - n_axis // 2) * x_in....  6.97 us
  transfers between devices with their start and end apart: 10, of which 6 were waited for; matrix products, arithmetic and copies ran while one was open for 15% of the time, Pallas kernels for 0%

profile of v1, /device:TPU:2, one launch (start us, length us, event | category | flops | bytes accessed | tf_op | source)
XLA Modules:
  0.0 342.1 jit_solution(15158532614868488669)
XLA Ops:
  7.3 13.0 %collective-permute-done = bf16[4,128,896]{2,1,0:T(8,128)(2,1)S(1)} collective-permute-done((bf16[4,128,896]{2,1,0:T(8,128)(2,1)}, bf16[4,128,896]{2,1,0:T(8,128)(2,1)S(1)}, u32[]{:S(2)}, u32[]{:S(2)}) %collective-permute-start) | collective-permute-done | bytes 917536 | tf_op jit(solution)/shard_map/ppermute | solution.py:17
  20.4 1.8 collective-permute-start.4
  22.1 11.0 %collective-permute-done.1 = bf16[4,128,896]{2,1,0:T(8,128)(2,1)S(1)} collective-permute-done((bf16[4,128,896]{2,1,0:T(8,128)(2,1)S(1)}, bf16[4,128,896]{2,1,0:T(8,128)(2,1)S(1)}, u32[]{:S(2)}, u32[]{:S(2)}) %collective-permute-start.1) | collective-permute-done | bytes 917536 | tf_op jit(solution)/shard_map/ppermute | solution.py:17
  34.0 1.7 collective-permute-start.5
  35.7 10.4 %collective-permute-done.2 = bf16[4,128,896]{2,1,0:T(8,128)(2,1)} collective-permute-done((bf16[4,128,896]{2,1,0:T(8,128)(2,1)S(1)}, bf16[4,128,896]{2,1,0:T(8,128)(2,1)}, u32[]{:S(2)}, u32[]{:S(2)}) %collective-permute-start.2) | collective-permute-done | bytes 917536 | tf_op jit(solution)/shard_map/ppermute | solution.py:17
  46.3 1.4 maximum_bitcast_fusion
  48.0 1.8 collective-permute-start.6
  49.8 9.4 %collective-permute-done.3 = bf16[4,128,896]{2,1,0:T(8,128)(2,1)} collective-permute-done((bf16[4,128,896]{2,1,0:T(8,128)(2,1)}, bf16[4,128,896]{2,1,0:T(8,128)(2,1)}, u32[]{:S(2)}, u32[]{:S(2)}) %collective-permute-start.3) | collective-permute-done | bytes 917536 | tf_op jit(solution)/shard_map/ppermute | solution.py:17
  59.2 2.2 constant_dynamic-update-slice_fusion.15
  61.4 2.2 constant_dynamic-update-slice_fusion.14
  63.6 1.0 constant_dynamic-update-slice_fusion.13
  67.7 2.2 constant_dynamic-update-slice_fusion.9
  69.9 1.0 constant_dynamic-update-slice_fusion.8
  70.9 2.2 constant_dynamic-update-slice_fusion.7
  73.1 2.2 constant_dynamic-update-slice_fusion.6
  76.3 1.0 constant_dynamic-update-slice_fusion.4
  79.4 2.2 constant_dynamic-update-slice_fusion.1
  81.6 1.0 constant_dynamic-update-slice_fusion
  82.6 7.0 %constant_dynamic-slice_fusion = bf16[32,128,896]{2,1,0:T(8,128)(2,1)} fusion(bf16[64,128,896]{2,1,0:T(8,128)(2,1)} %constant_dynamic-update-slice_fusion, s32[]{:T(128)S(6)} %select_n.42), kind=kLoop, calls=%fused_computation.50 | loop fusion | bytes 14680068 | tf_op jit(solution)/shard_map/jit(_roll_dynamic)/dynamic_slice | solution.py:21
  89.6 3.8 %gather_fusion = bf16[4,128,896]{2,1,0:T(8,128)(2,1)S(1)} fusion(bf16[32,128,896]{2,1,0:T(8,128)(2,1)} %constant_dynamic-slice_fusion, s32[1024]{0:T(1024)S(1)} %pad_clamp_fusion), kind=kCustom, calls=%fused_computation | custom fusion | bytes 1835024 | tf_op jit(solution)/shard_map/jit(_take)/gather | solution.py:42
  93.5 3.7 %collective-permute-start.7 = (bf16[256,896]{1,0:T(8,128)(2,1)S(1)}, bf16[256,896]{1,0:T(8,128)(2,1)S(1)}, u32[]{:S(2)}, u32[]{:S(2)}) collective-permute-start(bf16[256,896]{1,0:T(8,128)(2,1)S(1)} %bitcast.36), channel_id=1, source_target_pairs={{0,1},{1,2},{2,3},{4,5},{5,6},{6,7},{8,9},{9,10},{10,11},{12,13},{... | collective-permute-start | bytes 1376264 | tf_op jit(solution)/shard_map/ppermute | solution.py:29
  97.5 62.9 %all-gather.7.cloned.1.call-done = bf16[64,14,2048]{2,1,0:T(8,128)(2,1)} async-done(((bf16[1,14,2048]{2,1,0:T(8,128)(2,1)}), bf16[64,14,2048]{2,1,0:T(8,128)(2,1)}) %all-gather.7.cloned.1.call-update) | async-done | bytes 3670032 | tf_op jit(solution)/shard_map/all_gather | solution.py:46
  160.4 6.0 %reshape.75 = bf16[896,2048]{1,0:T(8,128)(2,1)} reshape(bf16[64,14,2048]{2,1,0:T(8,128)(2,1)} %all-gather.7.cloned.1.call-done) | data formatting | bytes 7340032
  166.4 6.0 %fusion.9 = bf16[96,8,16,128]{3,1,2,0:T(8,128)(2,1)S(1)} fusion(bf16[896,2048]{1,0:T(8,128)(2,1)} %reshape.75, bf16[512,896]{1,0:T(8,128)(2,1)S(1)} %bitcast_select_fusion, bf16[256,896]{1,0:T(8,128)(2,1)S(1)} %collective-permute-done.7), kind=kOutput, calls=%fused_computation.13 | convolution fusion | flops 2822897664 | bytes 8192000 | tf_op jit(solution)/shard_map/dot_general | solution.py:51
  173.4 1.2 fusion.3
  174.6 1.7 copy-done.1
  176.3 1.2 fusion.30
  177.5 132.1 %all-gather.5.cloned.1.call-done = bf16[64,14,2048]{2,1,0:T(8,128)(2,1)} async-done(((bf16[1,14,2048]{2,1,0:T(8,128)(2,1)}), bf16[64,14,2048]{2,1,0:T(8,128)(2,1)}) %all-gather.5.cloned.1.call-update) | async-done | bytes 3670032 | tf_op jit(solution)/shard_map/all_gather | solution.py:47
  309.6 6.0 %reshape.73 = bf16[896,2048]{1,0:T(8,128)(2,1)} reshape(bf16[64,14,2048]{2,1,0:T(8,128)(2,1)} %all-gather.5.cloned.1.call-done) | data formatting | bytes 7340032
  315.6 6.0 %fusion.8 = bf16[96,8,16,128]{3,1,2,0:T(8,128)(2,1)S(1)} fusion(bf16[896,2048]{1,0:T(8,128)(2,1)} %reshape.73, bf16[512,896]{1,0:T(8,128)(2,1)S(1)} %bitcast_select_fusion, bf16[256,896]{1,0:T(8,128)(2,1)S(1)} %collective-permute-done.7), kind=kOutput, calls=%fused_computation.12 | convolution fusion | flops 2822897664 | bytes 8192000 | tf_op jit(solution)/shard_map/dot_general | solution.py:54
  321.6 2.7 copy.19
  324.3 9.2 %fusion.15 = bf16[3,64,16,128]{3,1,2,0:T(8,128)(2,1)S(1)} fusion(bf16[3,256,16,128]{3,2,1,0:T(8,128)(2,1)} %bitcast.33, f32[3,16,64]{2,1,0:T(8,128)S(1)} %fusion.30, f32[3,16,64,256]{3,2,1,0:T(8,128)} %copy-done.1), kind=kOutput, calls=%fused_computation.18 | convolution fusion | flops 205655296 | bytes 7090176 | tf_op jit(solution)/shard_map/chqk,ckhd->cqhd/dot_general | solution.py:74
  (40 shorter events, 11.2 us)
Async XLA Ops:
  6.5 153.8 %all-gather.7.cloned.1.call-start = ((), (), s32[]{:S(2)}) async-start(), calls=%async_computation.1 | async-start | bytes 4259840 | tf_op jit(solution)/shard_map/all_gather | solution.py:46
  7.3 302.4 %all-gather.5.cloned.1.call-start = ((), (), s32[]{:S(2)}) async-start(), calls=%async_computation | async-start | bytes 4259840 | tf_op jit(solution)/shard_map/all_gather | solution.py:47
  7.3 13.0 %collective-permute-start = (bf16[4,128,896]{2,1,0:T(8,128)(2,1)}, bf16[4,128,896]{2,1,0:T(8,128)(2,1)S(1)}, u32[]{:S(2)}, u32[]{:S(2)}) collective-permute-start(bf16[4,128,896]{2,1,0:T(8,128)(2,1)} %param.7), channel_id=1, source_target_pairs={{0,4},{4,8},{8,12},{12,16},{16,20},{20,24},{24,28},{28,0},{1,5},{5... | collective-permute-start | bytes 2752520 | tf_op jit(solution)/shard_map/ppermute | solution.py:17
  20.3 12.8 %collective-permute-start.1 = (bf16[4,128,896]{2,1,0:T(8,128)(2,1)S(1)}, bf16[4,128,896]{2,1,0:T(8,128)(2,1)S(1)}, u32[]{:S(2)}, u32[]{:S(2)}) collective-permute-start(bf16[4,128,896]{2,1,0:T(8,128)(2,1)S(1)} %collective-permute-done), channel_id=1, source_target_pairs={{0,4},{4,8},{8,12},{12,16},{16,20},{20,24},{24,28},{28,0},{1,5},{5... | collective-permute-start | bytes 2752520 | tf_op jit(solution)/shard_map/ppermute | solution.py:17
  20.4 13.6 %collective-permute-start.4 = (bf16[4,128,896]{2,1,0:T(8,128)(2,1)}, bf16[4,128,896]{2,1,0:T(8,128)(2,1)S(1)}, u32[]{:S(2)}, u32[]{:S(2)}) collective-permute-start(bf16[4,128,896]{2,1,0:T(8,128)(2,1)} %param.7), channel_id=1, source_target_pairs={{0,28},{4,0},{8,4},{12,8},{16,12},{20,16},{24,20},{28,24},{1,29},{... | collective-permute-start | bytes 2752520 | tf_op jit(solution)/shard_map/ppermute | solution.py:19
  33.2 12.9 %collective-permute-start.2 = (bf16[4,128,896]{2,1,0:T(8,128)(2,1)S(1)}, bf16[4,128,896]{2,1,0:T(8,128)(2,1)}, u32[]{:S(2)}, u32[]{:S(2)}) collective-permute-start(bf16[4,128,896]{2,1,0:T(8,128)(2,1)S(1)} %collective-permute-done.1), channel_id=1, source_target_pairs={{0,4},{4,8},{8,12},{12,16},{16,20},{20,24},{24,28},{28,0},{1,5},{5... | collective-permute-start | bytes 2752520 | tf_op jit(solution)/shard_map/ppermute | solution.py:17
  34.0 14.1 %collective-permute-start.5 = (bf16[4,128,896]{2,1,0:T(8,128)(2,1)S(1)}, bf16[4,128,896]{2,1,0:T(8,128)(2,1)}, u32[]{:S(2)}, u32[]{:S(2)}) collective-permute-start(bf16[4,128,896]{2,1,0:T(8,128)(2,1)S(1)} %collective-permute-done.4), channel_id=1, source_target_pairs={{0,28},{4,0},{8,4},{12,8},{16,12},{20,16},{24,20},{28,24},{1,29},{... | collective-permute-start | bytes 2752520 | tf_op jit(solution)/shard_map/ppermute | solution.py:19
  46.1 13.1 %collective-permute-start.3 = (bf16[4,128,896]{2,1,0:T(8,128)(2,1)}, bf16[4,128,896]{2,1,0:T(8,128)(2,1)}, u32[]{:S(2)}, u32[]{:S(2)}) collective-permute-start(bf16[4,128,896]{2,1,0:T(8,128)(2,1)} %collective-permute-done.2), channel_id=1, source_target_pairs={{0,4},{4,8},{8,12},{12,16},{16,20},{20,24},{24,28},{28,0},{1,5},{5... | collective-permute-start | bytes 2752520 | tf_op jit(solution)/shard_map/ppermute | solution.py:17
  48.0 17.7 %copy-start = (bf16[4,128,896]{2,1,0:T(8,128)(2,1)S(1)}, bf16[4,128,896]{2,1,0:T(8,128)(2,1)}, u32[]{:S(2)}) copy-start(bf16[4,128,896]{2,1,0:T(8,128)(2,1)} %param.7) | copy-start | bytes 2752516
  48.0 21.9 %collective-permute-start.6 = (bf16[4,128,896]{2,1,0:T(8,128)(2,1)}, bf16[4,128,896]{2,1,0:T(8,128)(2,1)S(1)}, u32[]{:S(2)}, u32[]{:S(2)}) collective-permute-start(bf16[4,128,896]{2,1,0:T(8,128)(2,1)} %collective-permute-done.5), channel_id=1, source_target_pairs={{0,28},{4,0},{8,4},{12,8},{16,12},{20,16},{24,20},{28,24},{1,29},{... | collective-permute-start | bytes 2752520 | tf_op jit(solution)/shard_map/ppermute | solution.py:19
  93.5 72.8 %collective-permute-start.7 = (bf16[256,896]{1,0:T(8,128)(2,1)S(1)}, bf16[256,896]{1,0:T(8,128)(2,1)S(1)}, u32[]{:S(2)}, u32[]{:S(2)}) collective-permute-start(bf16[256,896]{1,0:T(8,128)(2,1)S(1)} %bitcast.36), channel_id=1, source_target_pairs={{0,1},{1,2},{2,3},{4,5},{5,6},{6,7},{8,9},{9,10},{10,11},{12,13},{... | collective-permute-start | bytes 1376264 | tf_op jit(solution)/shard_map/ppermute | solution.py:29
  174.6 1.7 copy-start.1
Sparse Core Ops, SparseCore 0:
  10.3 150.0 all-gather.6
  163.3 146.2 all-gather.4
